TPU v7x, 32 devices: a whole 2x2x4 slice. The times are simulated.
32 devices in a mesh: rep: 2 (over y), seq: 4 (over z), ch: 4 (over x, core).
Axes of the slice: x: 2, y: 2, z: 4, core: 2. Of those that a mesh axis runs over, the one named last changes fastest.
Arguments:
- key_proj: bfloat16 [4096, 4096], P(('rep', 'seq'), 'ch'), parts along dimension 0, may hold values from -6 to 6
- value_proj: bfloat16 [4096, 4096], P(('rep', 'seq'), 'ch'), parts along dimension 0, may hold values from -6 to 6
- query_proj: bfloat16 [4096, 4096], P(('rep', 'seq'), 'ch'), parts along dimension 0, may hold values from -6 to 6
- filters: bfloat16 [256, 2048], P('ch', 'seq'), may hold values from -3 to 3
- sources: int32 [8], P('rep'), parts along dimension 0, may hold values from 0 to 15, as said below
- owner: int32 [32], P('rep'), parts along dimension 0, may hold values from 0 to 3, as said below
Outputs:
- conv_out: bfloat16 [4096, 4096], P(('rep', 'seq'), 'ch'), parts along dimension 0
There are 2 independent parts, one for each index of `rep`. A program takes and returns all parts, laid end to end along the dimension named above; an argument that names none is the same for every part. Nothing has to cross between parts.
Inputs may be any that keep to these rules, and one draw needn't show every extreme that they name: `sources`: four distinct stretch numbers in increasing order; the first is 0 and the last 15. owner[k] is the index along seq of the shard holding stretch k; every shard holds exactly 4 stretches, stored one after another in increasing stretch number.
All inputs are finite; a program needn't handle non-finite values.
Results may differ from a plain program's by a relative error of at most 0.0049.
Values may be sent and summed in bfloat16 or wider, within the bound.
A program may use at most 64 MiB of HBM per device.

v0:
```python
import jax
import jax.numpy as jnp
from jax import lax
from jax.sharding import PartitionSpec as P

GROUP_CH = 16
STRETCH = 128
WIN = 4


def broadcast(x, axis, root):
    mine = lax.axis_index(axis) == root
    return lax.psum(jnp.where(mine, x, jnp.zeros_like(x)), axis)


def stretch_ranks(owner):
    numbers = jnp.arange(owner.shape[0], dtype=jnp.int32)
    same_owner = (owner[:, None] == owner[None, :]).astype(jnp.int32)
    earlier = (numbers[None, :] < numbers[:, None]).astype(jnp.int32)
    return jnp.sum(same_owner * earlier, axis=1)


def shards(key_proj, value_proj, query_proj, filters, sources, owner):
    row_count, channels = key_proj.shape
    slot_count = row_count // STRETCH
    group_count = channels // GROUP_CH
    myself = lax.axis_index("seq")
    numbers = jnp.arange(owner.shape[0], dtype=jnp.int32)
    stretch_rank = stretch_ranks(owner)
    source_hit = (sources[:, None] == numbers[None, :]).astype(jnp.int32)
    source_owner = jnp.sum(source_hit * owner[None, :], axis=1)
    source_slot = jnp.sum(source_hit * stretch_rank[None, :], axis=1)
    slot_numbers = jnp.arange(slot_count, dtype=jnp.int32)
    slot_hit = (
        (owner[None, :] == myself) & (stretch_rank[None, :] == slot_numbers[:, None])
    ).astype(jnp.int32)
    slot_stretch = jnp.sum(slot_hit * numbers[None, :], axis=1)

    def gated_piece(window_slot):
        row_start = source_slot[window_slot] * STRETCH
        key_rows = lax.dynamic_slice_in_dim(key_proj, row_start, STRETCH, 0)
        value_rows = lax.dynamic_slice_in_dim(value_proj, row_start, STRETCH, 0)
        return (key_rows.astype(jnp.float32) * value_rows.astype(jnp.float32)).astype(jnp.bfloat16)

    window = jnp.stack(
        [
            broadcast(gated_piece(window_slot), "seq", source_owner[window_slot])
            for window_slot in range(WIN)
        ]
    )
    lag_values = lax.all_gather(filters, "seq", axis=1, tiled=True)
    padded = jnp.concatenate(
        [jnp.zeros((group_count, STRETCH), lag_values.dtype), lag_values], axis=1
    )
    offsets = (
        STRETCH
        + jnp.arange(STRETCH, dtype=jnp.int32)[:, None]
        - jnp.arange(STRETCH, dtype=jnp.int32)[None, :]
    )
    pieces = window.reshape(WIN, STRETCH, group_count, GROUP_CH)

    def pair_term(target, window_slot):
        lag_block = target - sources[window_slot]
        lag_start = jnp.maximum(lag_block, 0) * STRETCH
        lag_span = lax.dynamic_slice_in_dim(padded, lag_start, 2 * STRETCH, 1)
        toeplitz = jnp.take(lag_span, offsets, axis=1)
        return jnp.einsum(
            "gij,jgc->igc", toeplitz, pieces[window_slot], preferred_element_type=jnp.float32
        )

    def one_slot(target_slot):
        target = slot_stretch[target_slot]
        summed = jnp.zeros((STRETCH, group_count, GROUP_CH), jnp.float32)
        for window_slot in range(WIN):
            causal = target >= sources[window_slot]

            def compute_term(target=target, window_slot=window_slot):
                return pair_term(target, window_slot)

            def empty_term():
                return jnp.zeros((STRETCH, group_count, GROUP_CH), jnp.float32)

            summed = summed + lax.cond(causal, compute_term, empty_term)
        return summed.reshape(STRETCH, channels)

    convolved = lax.map(one_slot, slot_numbers)
    return (query_proj.astype(jnp.float32) * convolved.reshape(row_count, channels)).astype(
        jnp.bfloat16
    )


def solution(mesh):
    return jax.shard_map(
        shards,
        mesh=mesh,
        in_specs=(
            P(("rep", "seq"), "ch"),
            P(("rep", "seq"), "ch"),
            P(("rep", "seq"), "ch"),
            P("ch", "seq"),
            P("rep"),
            P("rep"),
        ),
        out_specs=P(("rep", "seq"), "ch"),
        check_vma=False,
    )
```

profile of v0, /device:TPU:0, one launch (start us, length us, event | category | flops | bytes accessed | tf_op | source)
XLA Modules:
  0.0 944.0 jit_solution(11868660321685274857)
XLA Ops:
  6.5 0.9 select_reduce_fusion
  8.1 0.9 select_reduce_fusion.2
  14.7 2.0 fusion.47
  20.2 23.4 %all_gather.3 = bf16[64,2048]{0,1:T(8,128)(2,1)S(1)} all-gather(bf16[64,512]{0,1:T(8,128)(2,1)S(1)} %copy.21), channel_id=1, replica_groups=mesh['rep'=2,'seq'=4,'ch'=4] {'seq'}, dimensions={1}, use_global_device_ids=true | all-gather | bytes 327680 | tf_op jit(solution)/shard_map/all_gather | solution.py:51
  43.7 37.6 %all-reduce.4.cloned.1.call-done = (bf16[1,128,64,16]{1,3,2,0:T(8,128)(2,1)}, bf16[1,128,64,16]{1,3,2,0:T(8,128)(2,1)}, bf16[1,128,64,16]{1,3,2,0:T(8,128)(2,1)}, bf16[1,128,64,16]{1,3,2,0:T(8,128)(2,1)}) async-done(((bf16[1,128,64,16]{1,3,2,0:T(8,128)(2,1)}, bf16[1,128,64,16]{1,3,2,0:T(8,128)(2,1)}, bf16[1,128,64,16]{1,3,2,0:T(8,128)(2,1)}, bf16[1,128,64,16]{1,3,2,0:T(8,128)(2,1)}), ...) | async-done | bytes 1048592 | tf_op jit(solution)/shard_map/psum | solution.py:13
  81.3 2.3 pad_maximum_fusion
  83.6 850.3 %while.12 = (s32[]{:T(128)}, f32[4,128,1024]{2,1,0:T(8,128)}, s32[4]{0:T(128)S(1)}, s32[4]{0:T(128)S(1)}, s32[4]{0:T(128)S(1)}, /*index=5*/bf16[64,2176]{0,1:T(8...) while((s32[]{:T(128)}, f32[4,128,1024]{2,1,0:T(8,128)}, ...), condition=%wide.region_17.19_spmd.clone.clone, body=%wide.region_8.18_spmd.clone.clone.sunk | while | flops 139477024 | bytes 53544716 | solution.py:86
  90.0 65.4 %conditional.18 = (f32[128,64,16]{0,2,1:T(8,128)S(1)}) conditional(s32[]{:T(128)} %convert_element_type.128, () %tuple.90, (s32[4]{0:T(128)S(1)}, s32[]{:T(128)}, bf16[64,2176]{0,1:T(8,128)(2,1)S(1)}, s32[128,128]{1,0:T(8,128)S(1)}, bf16[4,128,64,16]{1,3,2,0:T(8,128)(2,1)}) %tuple.88), branch_computations={%region_9.9_spmd, %region_10.11_spmd} | conditional | flops 34766856 | bytes 11632722 | solution.py:83
  90.6 57.8 %gather_fusion = bf16[16384,64]{1,0:T(8,128)(2,1)} fusion(bf16[64,256]{0,1:T(8,128)(2,1)S(1)} %constant_dynamic-slice_fusion, s32[16384]{0:T(1024)S(1)} %bitcast_clamp_fusion), kind=kCustom, calls=%fused_computation.clone | custom fusion | bytes 4259840 | tf_op jit(solution)/shard_map/while/body/eval_jaxpr/cond/branch_1_fun/jit(_take)/gather | solution.py:66
  148.4 4.8 copy.17
  153.3 2.1 fusion.6
  156.6 68.3 %conditional.19 = (f32[128,64,16]{0,2,1:T(8,128)}) conditional(s32[]{:T(128)} %convert_element_type.129, () %tuple.91, (s32[4]{0:T(128)S(1)}, s32[]{:T(128)}, bf16[64,2176]{0,1:T(8,128)(2,1)}, s32[128,128]{1,0:T(8,128)S(1)}, bf16[4,128,64,16]{1,3,2,0:T(8,128)(2,1)}) %tuple.106), branch_computations={%region_11.12_spmd, %region_12.13_spmd} | conditional | flops 34766856 | bytes 11632730 | solution.py:83
  158.4 0.8 constant_dynamic-slice_fusion.1
  159.3 57.8 %gather_fusion.1 = bf16[16384,64]{1,0:T(8,128)(2,1)} fusion(bf16[64,256]{0,1:T(8,128)(2,1)S(1)} %constant_dynamic-slice_fusion.1, s32[16384]{0:T(1024)S(1)} %bitcast_clamp_fusion.1), kind=kCustom, calls=%fused_computation.1.clone | custom fusion | bytes 4259840 | tf_op jit(solution)/shard_map/while/body/eval_jaxpr/cond/branch_1_fun/jit(_take)/gather | solution.py:66
  217.1 4.8 copy.18
  222.0 3.0 fusion.17
  227.0 1.3 add_add_fusion.2
  234.5 66.5 %conditional.17 = (f32[128,64,16]{0,2,1:T(8,128)S(1)}) conditional(s32[]{:T(128)} %convert_element_type.127, () %tuple.89, (s32[4]{0:T(128)S(1)}, s32[]{:T(128)}, bf16[64,2176]{0,1:T(8,128)(2,1)S(1)}, s32[128,128]{1,0:T(8,128)S(1)}, bf16[4,128,64,16]{1,3,2,0:T(8,128)(2,1)}) %tuple.88), branch_computations={%region_13.14_spmd, %region_14.15_spmd} | conditional | flops 34766856 | bytes 11632730 | solution.py:83
  236.2 57.8 %gather_fusion.2 = bf16[16384,64]{1,0:T(8,128)(2,1)} fusion(bf16[64,256]{0,1:T(8,128)(2,1)S(1)} %constant_dynamic-slice_fusion.2, s32[16384]{0:T(1024)S(1)} %bitcast_clamp_fusion.2), kind=kCustom, calls=%fused_computation.2.clone | custom fusion | bytes 4259840 | tf_op jit(solution)/shard_map/while/body/eval_jaxpr/cond/branch_1_fun/jit(_take)/gather | solution.py:66
  294.1 4.8 copy.19
  298.9 2.1 fusion.28
  302.3 65.4 %conditional.18 = (f32[128,64,16]{0,2,1:T(8,128)S(1)}) conditional(s32[]{:T(128)} %convert_element_type.128, () %tuple.90, (s32[4]{0:T(128)S(1)}, s32[]{:T(128)}, bf16[64,2176]{0,1:T(8,128)(2,1)S(1)}, s32[128,128]{1,0:T(8,128)S(1)}, bf16[4,128,64,16]{1,3,2,0:T(8,128)(2,1)}) %tuple.88), branch_computations={%region_9.9_spmd, %region_10.11_spmd} | conditional | flops 34766856 | bytes 11632722 | solution.py:83
  302.9 57.8 %gather_fusion = bf16[16384,64]{1,0:T(8,128)(2,1)} fusion(bf16[64,256]{0,1:T(8,128)(2,1)S(1)} %constant_dynamic-slice_fusion, s32[16384]{0:T(1024)S(1)} %bitcast_clamp_fusion), kind=kCustom, calls=%fused_computation.clone | custom fusion | bytes 4259840 | tf_op jit(solution)/shard_map/while/body/eval_jaxpr/cond/branch_1_fun/jit(_take)/gather | solution.py:66
  360.7 4.8 copy.17
  365.6 2.1 fusion.6
  368.9 68.3 %conditional.19 = (f32[128,64,16]{0,2,1:T(8,128)}) conditional(s32[]{:T(128)} %convert_element_type.129, () %tuple.91, (s32[4]{0:T(128)S(1)}, s32[]{:T(128)}, bf16[64,2176]{0,1:T(8,128)(2,1)}, s32[128,128]{1,0:T(8,128)S(1)}, bf16[4,128,64,16]{1,3,2,0:T(8,128)(2,1)}) %tuple.106), branch_computations={%region_11.12_spmd, %region_12.13_spmd} | conditional | flops 34766856 | bytes 11632730 | solution.py:83
  370.7 0.8 constant_dynamic-slice_fusion.1
  371.6 57.8 %gather_fusion.1 = bf16[16384,64]{1,0:T(8,128)(2,1)} fusion(bf16[64,256]{0,1:T(8,128)(2,1)S(1)} %constant_dynamic-slice_fusion.1, s32[16384]{0:T(1024)S(1)} %bitcast_clamp_fusion.1), kind=kCustom, calls=%fused_computation.1.clone | custom fusion | bytes 4259840 | tf_op jit(solution)/shard_map/while/body/eval_jaxpr/cond/branch_1_fun/jit(_take)/gather | solution.py:66
  429.4 4.8 copy.18
  434.3 3.0 fusion.17
  439.3 1.3 add_add_fusion.2
  446.8 66.5 %conditional.17 = (f32[128,64,16]{0,2,1:T(8,128)S(1)}) conditional(s32[]{:T(128)} %convert_element_type.127, () %tuple.89, (s32[4]{0:T(128)S(1)}, s32[]{:T(128)}, bf16[64,2176]{0,1:T(8,128)(2,1)S(1)}, s32[128,128]{1,0:T(8,128)S(1)}, bf16[4,128,64,16]{1,3,2,0:T(8,128)(2,1)}) %tuple.88), branch_computations={%region_13.14_spmd, %region_14.15_spmd} | conditional | flops 34766856 | bytes 11632730 | solution.py:83
  448.5 57.8 %gather_fusion.2 = bf16[16384,64]{1,0:T(8,128)(2,1)} fusion(bf16[64,256]{0,1:T(8,128)(2,1)S(1)} %constant_dynamic-slice_fusion.2, s32[16384]{0:T(1024)S(1)} %bitcast_clamp_fusion.2), kind=kCustom, calls=%fused_computation.2.clone | custom fusion | bytes 4259840 | tf_op jit(solution)/shard_map/while/body/eval_jaxpr/cond/branch_1_fun/jit(_take)/gather | solution.py:66
  506.4 4.8 copy.19
  511.2 2.1 fusion.28
  514.6 65.4 %conditional.18 = (f32[128,64,16]{0,2,1:T(8,128)S(1)}) conditional(s32[]{:T(128)} %convert_element_type.128, () %tuple.90, (s32[4]{0:T(128)S(1)}, s32[]{:T(128)}, bf16[64,2176]{0,1:T(8,128)(2,1)S(1)}, s32[128,128]{1,0:T(8,128)S(1)}, bf16[4,128,64,16]{1,3,2,0:T(8,128)(2,1)}) %tuple.88), branch_computations={%region_9.9_spmd, %region_10.11_spmd} | conditional | flops 34766856 | bytes 11632722 | solution.py:83
  515.2 57.8 %gather_fusion = bf16[16384,64]{1,0:T(8,128)(2,1)} fusion(bf16[64,256]{0,1:T(8,128)(2,1)S(1)} %constant_dynamic-slice_fusion, s32[16384]{0:T(1024)S(1)} %bitcast_clamp_fusion), kind=kCustom, calls=%fused_computation.clone | custom fusion | bytes 4259840 | tf_op jit(solution)/shard_map/while/body/eval_jaxpr/cond/branch_1_fun/jit(_take)/gather | solution.py:66
  573.0 4.8 copy.17
  577.9 2.1 fusion.6
  581.2 68.3 %conditional.19 = (f32[128,64,16]{0,2,1:T(8,128)}) conditional(s32[]{:T(128)} %convert_element_type.129, () %tuple.91, (s32[4]{0:T(128)S(1)}, s32[]{:T(128)}, bf16[64,2176]{0,1:T(8,128)(2,1)}, s32[128,128]{1,0:T(8,128)S(1)}, bf16[4,128,64,16]{1,3,2,0:T(8,128)(2,1)}) %tuple.106), branch_computations={%region_11.12_spmd, %region_12.13_spmd} | conditional | flops 34766856 | bytes 11632730 | solution.py:83
  583.0 0.8 constant_dynamic-slice_fusion.1
  583.9 57.8 %gather_fusion.1 = bf16[16384,64]{1,0:T(8,128)(2,1)} fusion(bf16[64,256]{0,1:T(8,128)(2,1)S(1)} %constant_dynamic-slice_fusion.1, s32[16384]{0:T(1024)S(1)} %bitcast_clamp_fusion.1), kind=kCustom, calls=%fused_computation.1.clone | custom fusion | bytes 4259840 | tf_op jit(solution)/shard_map/while/body/eval_jaxpr/cond/branch_1_fun/jit(_take)/gather | solution.py:66
  641.7 4.8 copy.18
  646.6 3.0 fusion.17
  651.6 1.3 add_add_fusion.2
  659.1 66.5 %conditional.17 = (f32[128,64,16]{0,2,1:T(8,128)S(1)}) conditional(s32[]{:T(128)} %convert_element_type.127, () %tuple.89, (s32[4]{0:T(128)S(1)}, s32[]{:T(128)}, bf16[64,2176]{0,1:T(8,128)(2,1)S(1)}, s32[128,128]{1,0:T(8,128)S(1)}, bf16[4,128,64,16]{1,3,2,0:T(8,128)(2,1)}) %tuple.88), branch_computations={%region_13.14_spmd, %region_14.15_spmd} | conditional | flops 34766856 | bytes 11632730 | solution.py:83
  660.9 57.8 %gather_fusion.2 = bf16[16384,64]{1,0:T(8,128)(2,1)} fusion(bf16[64,256]{0,1:T(8,128)(2,1)S(1)} %constant_dynamic-slice_fusion.2, s32[16384]{0:T(1024)S(1)} %bitcast_clamp_fusion.2), kind=kCustom, calls=%fused_computation.2.clone | custom fusion | bytes 4259840 | tf_op jit(solution)/shard_map/while/body/eval_jaxpr/cond/branch_1_fun/jit(_take)/gather | solution.py:66
  718.7 4.8 copy.19
  723.5 2.1 fusion.28
  726.9 65.4 %conditional.18 = (f32[128,64,16]{0,2,1:T(8,128)S(1)}) conditional(s32[]{:T(128)} %convert_element_type.128, () %tuple.90, (s32[4]{0:T(128)S(1)}, s32[]{:T(128)}, bf16[64,2176]{0,1:T(8,128)(2,1)S(1)}, s32[128,128]{1,0:T(8,128)S(1)}, bf16[4,128,64,16]{1,3,2,0:T(8,128)(2,1)}) %tuple.88), branch_computations={%region_9.9_spmd, %region_10.11_spmd} | conditional | flops 34766856 | bytes 11632722 | solution.py:83
  727.5 57.8 %gather_fusion = bf16[16384,64]{1,0:T(8,128)(2,1)} fusion(bf16[64,256]{0,1:T(8,128)(2,1)S(1)} %constant_dynamic-slice_fusion, s32[16384]{0:T(1024)S(1)} %bitcast_clamp_fusion), kind=kCustom, calls=%fused_computation.clone | custom fusion | bytes 4259840 | tf_op jit(solution)/shard_map/while/body/eval_jaxpr/cond/branch_1_fun/jit(_take)/gather | solution.py:66
  785.3 4.8 copy.17
  790.2 2.1 fusion.6
  793.5 68.3 %conditional.19 = (f32[128,64,16]{0,2,1:T(8,128)}) conditional(s32[]{:T(128)} %convert_element_type.129, () %tuple.91, (s32[4]{0:T(128)S(1)}, s32[]{:T(128)}, bf16[64,2176]{0,1:T(8,128)(2,1)}, s32[128,128]{1,0:T(8,128)S(1)}, bf16[4,128,64,16]{1,3,2,0:T(8,128)(2,1)}) %tuple.106), branch_computations={%region_11.12_spmd, %region_12.13_spmd} | conditional | flops 34766856 | bytes 11632730 | solution.py:83
  796.2 57.8 %gather_fusion.1 = bf16[16384,64]{1,0:T(8,128)(2,1)} fusion(bf16[64,256]{0,1:T(8,128)(2,1)S(1)} %constant_dynamic-slice_fusion.1, s32[16384]{0:T(1024)S(1)} %bitcast_clamp_fusion.1), kind=kCustom, calls=%fused_computation.1.clone | custom fusion | bytes 4259840 | tf_op jit(solution)/shard_map/while/body/eval_jaxpr/cond/branch_1_fun/jit(_take)/gather | solution.py:66
  854.0 4.8 copy.18
  858.9 3.0 fusion.17
  863.1 68.4 %conditional.16 = (f32[128,64,16]{0,2,1:T(8,128)}) conditional(s32[]{:T(128)} %convert_element_type.126, () %tuple.87, (s32[4]{0:T(128)S(1)}, s32[]{:T(128)}, bf16[64,2176]{0,1:T(8,128)(2,1)}, s32[128,128]{1,0:T(8,128)S(1)}, bf16[4,128,64,16]{1,3,2,0:T(8,128)(2,1)}) %tuple.107), branch_computations={%region_15.16_spmd, %region_16.17_spmd} | conditional | flops 34766856 | bytes 11632730 | solution.py:83
  865.0 0.8 constant_dynamic-slice_fusion.3
  865.9 57.8 %gather_fusion.3 = bf16[16384,64]{1,0:T(8,128)(2,1)} fusion(bf16[64,256]{0,1:T(8,128)(2,1)S(1)} %constant_dynamic-slice_fusion.3, s32[16384]{0:T(1024)S(1)} %bitcast_clamp_fusion.3), kind=kCustom, calls=%fused_computation.3.clone | custom fusion | bytes 4259840 | tf_op jit(solution)/shard_map/while/body/eval_jaxpr/cond/branch_1_fun/jit(_take)/gather | solution.py:66
  923.7 4.8 copy.20
  928.6 3.0 fusion.39
  931.5 1.3 add_add_fusion.2
  933.9 3.2 fusion.46
  (105 shorter events, 28.7 us)
Async XLA Ops:
  6.5 74.8 %all-reduce.4.cloned.1.call-start = ((), (), s32[]{:S(2)}) async-start(), calls=%async_computation | async-start | bytes 2097152 | tf_op jit(solution)/shard_map/psum | solution.py:13
  16.7 3.4 copy-start.3
  20.1 63.6 %copy-start.2 = (s32[4]{0:T(128)S(1)}, s32[4]{0:T(128)}, u32[]{:S(2)}) copy-start(s32[4]{0:T(128)} %param.22) | copy-start | bytes 52
  83.6 6.3 copy-start
  228.4 1.1 copy-start.1
  229.4 72.9 %copy-start = (bf16[64,2176]{0,1:T(8,128)(2,1)}, bf16[64,2176]{0,1:T(8,128)(2,1)S(1)}, u32[]{:S(2)}) copy-start(bf16[64,2176]{0,1:T(8,128)(2,1)S(1)} %get-tuple-element.298) | copy-start | bytes 835588 | tf_op jit(solution)/shard_map/while
  440.7 1.1 copy-start.1
  441.7 72.9 %copy-start = (bf16[64,2176]{0,1:T(8,128)(2,1)}, bf16[64,2176]{0,1:T(8,128)(2,1)S(1)}, u32[]{:S(2)}) copy-start(bf16[64,2176]{0,1:T(8,128)(2,1)S(1)} %get-tuple-element.298) | copy-start | bytes 835588 | tf_op jit(solution)/shard_map/while
  653.0 1.1 copy-start.1
  654.0 72.9 %copy-start = (bf16[64,2176]{0,1:T(8,128)(2,1)}, bf16[64,2176]{0,1:T(8,128)(2,1)S(1)}, u32[]{:S(2)}) copy-start(bf16[64,2176]{0,1:T(8,128)(2,1)S(1)} %get-tuple-element.298) | copy-start | bytes 835588 | tf_op jit(solution)/shard_map/while
  932.9 1.1 copy-start.1
Sparse Core Ops, SparseCore 0:
  20.2 61.0 all-reduce.3
where the time goes:
time: 946 us; the launch traced here: 944 us
  local copies, waits for them, and re-layouts  780 us (82%)
  loops' own time  39.1 us (4%)
  waiting for transfers between devices  37.6 us (4%)
  matrix products  29.7 us (3%)
  blocking collectives  23.4 us (2%)
  between operations  18.5 us (2%)
  other arithmetic  16 us (2%)
    gather x24, local copies, waits for them, and re-layouts, pair_term(): toeplitz = jnp.take(lag_span, offsets, axis=1)  752 us
    psum x1, waiting for transfers between devices, broadcast(): return lax.psum(jnp.where(mine, x, jnp.zeros_like(x)), axis)  37.6 us
    dot_general x12, matrix products, pair_term(): jnp.einsum('gij,jgc->igc', toeplitz, pieces[window_slot], preferred_eleme...  29.7 us
    another operation x1, loops' own time, shards(): convolved = lax.map(one_slot, slot_numbers)  26.9 us
    all_gather x1, blocking collectives, shards(): lag_values = lax.all_gather(filters, 'seq', axis=1, tiled=True)  23.4 us
  transfers between devices with their start and end apart: 1, of which 1 were waited for; matrix products, arithmetic and copies ran while one was open for 0% of the time, Pallas kernels for 0%

commit v1 on v0

v1 whole, which is shorter than its diff:
```python
import jax
import jax.numpy as jnp
from jax import lax
from jax.experimental import pallas as pl
from jax.experimental.pallas import tpu as pltpu
from jax.sharding import PartitionSpec as P

GROUP_CH = 16
STRETCH = 128
WIN = 4
PIECE = 16
OCT = 8
F32 = jnp.float32
BF16 = jnp.bfloat16


def lane_block(rows):
    return lax.broadcasted_iota(jnp.int32, (rows, 128), 1) // PIECE


def block_transpose(parts):
    parts = list(parts)
    block = lane_block(parts[0].shape[0])
    for step in (1, 2, 4):
        keep = (block & step) == 0
        for p in range(OCT):
            if p & step:
                continue
            low, high = parts[p], parts[p + step]
            parts[p] = jnp.where(keep, low, pltpu.roll(high, PIECE * step, 1))
            parts[p + step] = jnp.where(keep, pltpu.roll(low, 128 - PIECE * step, 1), high)
    return parts


def unrolled_columns(piece):
    block = lane_block(PIECE)
    rows = [None] * 16
    zero = jnp.zeros_like(piece)
    for j in range(OCT):
        turned = pltpu.roll(piece, PIECE * j, 1) if j else piece
        rows[7 - j] = jnp.where(block >= j, turned, zero).astype(BF16)
        rows[15 - j] = jnp.where(block < j, turned, zero).astype(BF16)
    return jnp.concatenate(rows, axis=0)


def shifted_filters(filters_ref, g_ref, padded_ref, stretches):
    groups = filters_ref.shape[0]
    width = padded_ref.shape[1]
    row = lax.broadcasted_iota(jnp.int32, (128, 128), 0)
    col = lax.broadcasted_iota(jnp.int32, (128, 128), 1)
    flip = (row + col == 127).astype(BF16)
    for n in range(stretches):
        chunk = filters_ref[:, 128 * (stretches - 1 - n) : 128 * (stretches - n)]
        padded_ref[:, 128 * n : 128 * (n + 1)] = jnp.dot(chunk, flip, preferred_element_type=F32)
    padded_ref[:, 128 * stretches :] = jnp.zeros((groups, width - 128 * stretches), F32)
    for g in range(groups):
        spread = jnp.broadcast_to(padded_ref[g : g + 1, :], (PIECE, width))
        turned = pltpu.roll(spread, width - 15, 1, stride=1, stride_axis=0).astype(BF16)
        for n in range(stretches + 2):
            g_ref[g, n] = turned[:, 128 * n : 128 * (n + 1)]


def conv_kernel(
    sources_ref, owner_ref, key_ref, value_ref, query_ref, window_ref, filters_ref,
    out_ref, g_ref, padded_ref, slot_ref,
):
    stretches = owner_ref.shape[0]
    slots = key_ref.shape[0] // STRETCH
    me = lax.axis_index("seq")
    last = stretches - 1
    count = jnp.int32(0)
    for k in range(stretches):
        slot_ref[count] = k
        count = count + jnp.where(owner_ref[k] == me, 1, 0)

    shifted_filters(filters_ref, g_ref, padded_ref, stretches)

    own_last = owner_ref[last] == me
    local = key_ref[(slots - 1) * STRETCH :, :].astype(F32) * value_ref[
        (slots - 1) * STRETCH :, :
    ].astype(F32)
    local = jnp.where(own_last, local.astype(BF16).astype(F32), 0.0)

    pieces = []
    for w in range(WIN):
        rows = local if w == WIN - 1 else window_ref[w].astype(F32)
        pieces.append(
            block_transpose([rows[PIECE * e : PIECE * (e + 1), :] for e in range(OCT)])
        )
    firsts = []
    for t in range(slots):
        target = slot_ref[t]
        firsts.append(
            [last - jnp.maximum(target - sources_ref[w], -1) for w in range(WIN)]
        )
    results = []
    for g in range(OCT):
        columns = jnp.concatenate([unrolled_columns(pieces[w][g]) for w in range(WIN)], axis=0)
        taps = jnp.concatenate(
            [
                jnp.concatenate(
                    [g_ref[g, firsts[t][w] + half] for w in range(WIN) for half in range(2)],
                    axis=1,
                )
                for t in range(slots)
            ],
            axis=0,
        )
        results.append(jnp.dot(taps, columns, preferred_element_type=F32))
    for t in range(slots):
        rows = block_transpose(
            [results[g][PIECE * t : PIECE * (t + 1), :] for g in range(OCT)]
        )
        for a in range(OCT):
            at = slice(STRETCH * t + PIECE * a, STRETCH * t + PIECE * (a + 1))
            out_ref[at, :] = (query_ref[at, :].astype(F32) * rows[a]).astype(BF16)


def conv(key_proj, value_proj, query_proj, window, filters, sources, owner):
    rows, channels = key_proj.shape
    groups, lags = filters.shape
    stretches = owner.shape[0]
    slots = rows // STRETCH
    wide = pl.BlockSpec((rows, 128), lambda o, *_: (0, o))
    return pl.pallas_call(
        conv_kernel,
        out_shape=jax.ShapeDtypeStruct((rows, channels), BF16),
        grid_spec=pltpu.PrefetchScalarGridSpec(
            num_scalar_prefetch=2,
            grid=(channels // 128,),
            in_specs=[
                wide,
                wide,
                wide,
                pl.BlockSpec((WIN - 1, STRETCH, 128), lambda o, *_: (0, 0, o)),
                pl.BlockSpec((OCT, lags), lambda o, *_: (o, 0)),
            ],
            out_specs=wide,
            scratch_shapes=[
                pltpu.VMEM((OCT, stretches + 2, PIECE, 128), BF16),
                pltpu.VMEM((OCT, lags + 256), F32),
                pltpu.SMEM((slots + 1,), jnp.int32),
            ],
        ),
        compiler_params=pltpu.CompilerParams(vmem_limit_bytes=48 * 2**20),
        cost_estimate=pl.CostEstimate(flops=2**30, bytes_accessed=6 * 2**20, transcendentals=0),
    )(sources, owner, key_proj, value_proj, query_proj, window, filters)


def shards(key_proj, value_proj, query_proj, filters, sources, owner):
    myself = lax.axis_index("seq")
    stretches = owner.shape[0]
    numbers = jnp.arange(stretches, dtype=jnp.int32)
    parts = []
    for w in range(WIN - 1):
        source = sources[w]
        hit = numbers == source
        source_owner = jnp.sum(jnp.where(hit, owner, 0))
        slot = jnp.sum(jnp.where((owner == source_owner) & (numbers < source), 1, 0))
        start = slot * STRETCH
        keys = lax.dynamic_slice_in_dim(key_proj, start, STRETCH, 0).astype(F32)
        values = lax.dynamic_slice_in_dim(value_proj, start, STRETCH, 0).astype(F32)
        gated = (keys * values).astype(BF16)
        parts.append(jnp.where(source_owner == myself, gated, jnp.zeros_like(gated)))
    window = lax.psum(jnp.stack(parts), "seq")
    lag_values = lax.all_gather(filters, "seq", axis=1, tiled=True)
    return conv(key_proj, value_proj, query_proj, window, lag_values, sources, owner)


def solution(mesh):
    return jax.shard_map(
        shards,
        mesh=mesh,
        in_specs=(
            P(("rep", "seq"), "ch"),
            P(("rep", "seq"), "ch"),
            P(("rep", "seq"), "ch"),
            P("ch", "seq"),
            P("rep"),
            P("rep"),
        ),
        out_specs=P(("rep", "seq"), "ch"),
        check_vma=False,
    )
```

time: 946 us -> 92 us (0.10)
  local copies, waits for them, and re-layouts: 780 us -> 3.92 us
  loops' own time: 39.1 us -> 0 us
  matrix products: 29.7 us -> 0 us
  Pallas kernels: 0 us -> 11.9 us
    gather x24 -> x0, local copies, waits for them, and re-layouts: 752 us -> none  [pair_term(): toeplitz = jnp.take(lag_span, offsets, axis=1)]
    another operation x17 -> x0, loops' own time: 39.1 us -> none  [the longest x1 26.9 us: shards(): convolved = lax.map(one_slot, slot_numbers)]
    dot_general x12 -> x0, matrix products: 29.7 us -> none  [pair_term(): jnp.einsum('gij,jgc->igc', toeplitz, pieces[window_slot], preferred_eleme...]
    pallas_call x0 -> x1, Pallas kernels: none -> 11.9 us  [conv(): pl.pallas_call(conv_kernel, out_shape=jax.ShapeDtypeStruct((rows, channel...]
    dynamic_slice x20 -> x0, local copies, waits for them, and re-layouts: 9.66 us -> none  [the longest x12 4.33 us: pair_term(): lag_span = lax.dynamic_slice_in_dim(padded, lag_start, 2 * STRETCH, 1)]
where the time goes in v1:
time: 92 us; the launch traced here: 91.7 us
  waiting for transfers between devices  31.1 us (34%)
  blocking collectives  17.3 us (19%)
  between operations  17.1 us (19%)
  Pallas kernels  11.9 us (13%)
  other arithmetic  10.3 us (11%)
  local copies, waits for them, and re-layouts  3.92 us (4%)
    psum x1, waiting for transfers between devices, shards(): window = lax.psum(jnp.stack(parts), 'seq')  31.1 us
    all_gather x1, blocking collectives, shards(): lag_values = lax.all_gather(filters, 'seq', axis=1, tiled=True)  17.3 us
    pallas_call x1, Pallas kernels, conv(): pl.pallas_call(conv_kernel, out_shape=jax.ShapeDtypeStruct((rows, channel...  11.9 us
    reduce_sum x2, other arithmetic, shards(): jnp.sum(jnp.where((owner == source_owner) & (numbers < source), 1, 0))  5.71 us
    unnamed x14, local copies, waits for them, and re-layouts  3.27 us
    another operation x2, other arithmetic, shards(): window = lax.psum(jnp.stack(parts), 'seq')  2.71 us
    reduce_sum x1, other arithmetic, shards(): source_owner = jnp.sum(jnp.where(hit, owner, 0))  1.92 us
  transfers between devices with their start and end apart: 1, of which 1 were waited for; matrix products, arithmetic and copies ran while one was open for 0% of the time, Pallas kernels for 0%

profile of v1, /device:TPU:0, one launch (start us, length us, event | category | flops | bytes accessed | tf_op | source)
XLA Modules:
  0.0 91.7 jit_solution(685678416544321669)
XLA Ops:
  6.5 0.0 all-reduce.2.cloned.1.call-start
  6.5 0.0 copy-start.4
  6.5 0.7 copy-done.4
  7.2 0.6 fusion.12
  7.8 0.0 copy-start.5
  7.8 0.7 copy-done.5
  8.5 1.9 %fusion.6 = (s32[]{:T(128)}, s32[]{:T(128)}) fusion(s32[16]{0:T(128)S(1)} %copy-done.5, s32[]{:T(128)} %bitcast, s32[]{:T(128)} %bitcast.2), kind=kLoop, calls=%fused_computation.16 | loop fusion | flops 94 | bytes 80 | tf_op jit(solution)/shard_map/reduce_sum | solution.py:158
  11.7 3.8 %fusion.11 = (s32[]{:T(128)}, s32[]{:T(128)}, s32[]{:T(128)}) fusion(s32[16]{0:T(128)S(1)} %copy-done.5, s32[]{:T(128)} %get-tuple-element.8, s32[]{:T(128)} %bitcast, s32[]{:T(128)} %bitcast.4, s32[]{:T(128)} %bitcast.2, s32[]{:T(128)} %get-tuple-element.9), kind=kLoop, calls=%fused_computation.21 | loop fusion | flops 205 | bytes 96 | tf_op jit(solution)/shard_map/reduce_sum | solution.py:159
  16.1 1.9 %fusion.9 = s32[]{:T(128)} fusion(s32[16]{0:T(128)S(1)} %copy-done.5, s32[]{:T(128)} %get-tuple-element.6, s32[]{:T(128)} %bitcast.4), kind=kLoop, calls=%fused_computation.19 | loop fusion | flops 79 | bytes 76 | tf_op jit(solution)/shard_map/reduce_sum | solution.py:159
  19.8 0.0 copy-start.2
  19.8 1.7 %fusion.1 = (bf16[1,128,1024]{2,1,0:T(8,128)(2,1)S(1)}, bf16[1,128,1024]{2,1,0:T(8,128)(2,1)S(1)}, bf16[1,128,1024]{2,1,0:T(8,128)(2,1)S(1)}) fusion(bf16[512,1024]{1,0:T(8,128)(2,1)} %value_ref.1, s32[]{:T(128)S(6)} %select_n.55, bf16[512,1024]{1,0:T(8,128)(2,1)} %key_ref.1, pred[]{:T(512)S(6)} %eq.47, s32[]{:T(128)S(6)} %select_n.60, pred[]{:T(512)S(6)} %eq.52, ...), kind=kLoop, calls=%fused_computation.5 | loop fusion | flops 1966080 | bytes 2359311 | tf_op jit(solution)/shard_map/stack | solution.py:165
  21.6 0.0 copy-start
  21.6 0.0 copy-start.1
  21.6 1.0 %pad_maximum_fusion = bf16[3,128,1024]{2,1,0:T(8,128)(2,1)} fusion(bf16[1,128,1024]{2,1,0:T(8,128)(2,1)S(1)} %get-tuple-element.12, bf16[1,128,1024]{2,1,0:T(8,128)(2,1)S(1)} %get-tuple-element.11, bf16[1,128,1024]{2,1,0:T(8,128)(2,1)S(1)} %get-tuple-element.10), kind=kLoop, calls=%fused_computation | loop fusion | flops 786432 | bytes 1572864 | tf_op jit(solution)/shard_map/stack | solution.py:165
  22.6 0.0 copy-start.6
  22.6 0.0 all-reduce.2.cloned.1.call-update
  22.6 0.8 copy-done.6
  23.4 17.3 %all_gather.3.filters_ref = bf16[64,2048]{1,0:T(8,128)(2,1)S(1)} all-gather(bf16[64,512]{1,0:T(8,128)(2,1)S(1)} %copy-done.6), channel_id=1, replica_groups=mesh['rep'=2,'seq'=4,'ch'=4] {'seq'}, dimensions={1}, use_global_device_ids=true | all-gather | bytes 327680 | tf_op jit(solution)/shard_map/all_gather | solution.py:166
  40.7 31.1 %all-reduce.2.cloned.1.call-done.window_ref = bf16[3,128,1024]{2,1,0:T(8,128)(2,1)} async-done(((bf16[3,128,1024]{2,1,0:T(8,128)(2,1)}), bf16[3,128,1024]{2,1,0:T(8,128)(2,1)}) %all-reduce.2.cloned.1.call-update) | async-done | bytes 786448 | tf_op jit(solution)/shard_map/psum | solution.py:165
  71.8 0.0 copy-done.2
  71.8 0.0 copy-done
  71.8 0.0 copy-done.1
  71.8 0.0 copy-start.3
  71.8 1.1 %copy-done.3 = bf16[3,128,1024]{2,1,0:T(8,128)(2,1)S(1)} copy-done((bf16[3,128,1024]{2,1,0:T(8,128)(2,1)S(1)}, bf16[3,128,1024]{2,1,0:T(8,128)(2,1)}, u32[]{:S(2)}) %copy-start.3) | copy-done | bytes 786456
  73.0 11.9 %shard_map.64 = bf16[512,1024]{1,0:T(8,128)(2,1)} custom-call(s32[4]{0:T(128)S(1)} %copy-done.4, s32[16]{0:T(128)S(1)} %copy-done.5, bf16[512,1024]{1,0:T(8,128)(2,1)S(1)} %copy-done, bf16[512,1024]{1,0:T(8,128)(2,1)S(1)} %copy-done.1, bf16[512,1024]{1,0:T(8,128)(2,1)S(1)} %copy-done.2, bf16[3,128,1024]{2,1,0:T(8,128)(2,1)S(1)} %copy-done.3, ...), custom_call_target="tpu_custom_call" | custom-call | flops 1073741824 | bytes 6291456 | tf_op jit(solution)/shard_map/pallas_call | solution.py:125
Async XLA Ops:
  6.5 65.3 %all-reduce.2.cloned.1.call-start = ((), (), s32[]{:S(2)}) async-start(), calls=%async_computation | async-start | bytes 1572864 | tf_op jit(solution)/shard_map/psum | solution.py:165
  6.5 0.7 copy-start.4
  7.8 0.7 copy-start.5
  19.8 52.0 %copy-start.2 = (bf16[512,1024]{1,0:T(8,128)(2,1)S(1)}, bf16[512,1024]{1,0:T(8,128)(2,1)}, u32[]{:S(2)}) copy-start(bf16[512,1024]{1,0:T(8,128)(2,1)} %query_ref.1) | copy-start | bytes 3145732
  21.6 50.2 %copy-start = (bf16[512,1024]{1,0:T(8,128)(2,1)S(1)}, bf16[512,1024]{1,0:T(8,128)(2,1)}, u32[]{:S(2)}) copy-start(bf16[512,1024]{1,0:T(8,128)(2,1)} %key_ref.1) | copy-start | bytes 3145732
  21.6 50.2 %copy-start.1 = (bf16[512,1024]{1,0:T(8,128)(2,1)S(1)}, bf16[512,1024]{1,0:T(8,128)(2,1)}, u32[]{:S(2)}) copy-start(bf16[512,1024]{1,0:T(8,128)(2,1)} %value_ref.1) | copy-start | bytes 3145732
  22.6 0.8 copy-start.6
  71.8 1.1 %copy-start.3 = (bf16[3,128,1024]{2,1,0:T(8,128)(2,1)S(1)}, bf16[3,128,1024]{2,1,0:T(8,128)(2,1)}, u32[]{:S(2)}) copy-start(bf16[3,128,1024]{2,1,0:T(8,128)(2,1)} %all-reduce.2.cloned.1.call-done.window_ref) | copy-start | bytes 2359300
Sparse Core Ops, SparseCore 0:
  22.7 49.0 all-reduce.1

commit v2 on v1

v2 whole, which is shorter than its diff:
```python
import functools

import jax
import jax.numpy as jnp
from jax import lax
from jax.experimental import pallas as pl
from jax.experimental.pallas import tpu as pltpu
from jax.sharding import PartitionSpec as P

GROUP_CH = 16
STRETCH = 128
WIN = 4
PIECE = 16
OCT = 8
F32 = jnp.float32
BF16 = jnp.bfloat16


def lane_block(rows):
    return lax.broadcasted_iota(jnp.int32, (rows, 128), 1) // PIECE


def block_transpose(parts):
    parts = list(parts)
    block = lane_block(parts[0].shape[0])
    for step in (1, 2, 4):
        keep = (block & step) == 0
        for p in range(OCT):
            if p & step:
                continue
            low, high = parts[p], parts[p + step]
            parts[p] = jnp.where(keep, low, pltpu.roll(high, PIECE * step, 1))
            parts[p + step] = jnp.where(keep, pltpu.roll(low, 128 - PIECE * step, 1), high)
    return parts


def unrolled_columns(piece):
    block = lane_block(PIECE)
    rows = [None] * 16
    zero = jnp.zeros_like(piece)
    for j in range(OCT):
        turned = pltpu.roll(piece, PIECE * j, 1) if j else piece
        rows[7 - j] = jnp.where(block >= j, turned, zero).astype(BF16)
        rows[15 - j] = jnp.where(block < j, turned, zero).astype(BF16)
    return jnp.concatenate(rows, axis=0)


def turn_filters(shards_ref, padded_ref):
    count, groups, span = shards_ref.shape
    width = padded_ref.shape[1]
    lags = count * span
    row = lax.broadcasted_iota(jnp.int32, (128, 128), 0)
    col = lax.broadcasted_iota(jnp.int32, (128, 128), 1)
    flip = (row + col == 127).astype(BF16)
    for n in range(lags // 128):
        at = lags - 128 * (n + 1)
        chunk = shards_ref[at // span, :, at % span : at % span + 128]
        padded_ref[:, 128 * n : 128 * (n + 1)] = jnp.dot(chunk, flip, preferred_element_type=F32)
    padded_ref[:, lags:] = jnp.zeros((groups, width - lags), F32)


def fused_kernel(
    size, sources_ref, owner_ref, key_ref, value_ref, query_ref, filters_ref,
    out_ref, right_ref, left_ref, from_left_ref, from_right_ref, taps_ref, padded_ref, g_ref,
    own_sem, tap_right_send, tap_left_send, tap_recv,
    right_send, right_recv, left_send, left_recv,
):
    stretches = owner_ref.shape[0]
    slots = key_ref.shape[0]
    octets = key_ref.shape[2] // 128
    width = padded_ref.shape[1]
    last = stretches - 1
    me = lax.axis_index("seq")
    has_left = me > 0
    has_right = me < size - 1

    def hop(src, dst, send, recv, step):
        return pltpu.make_async_remote_copy(
            src_ref=src, dst_ref=dst, send_sem=send, recv_sem=recv,
            device_id={"seq": me + step}, device_id_type=pl.DeviceIdType.MESH,
        )

    def tap_hop(shard, step):
        send = tap_right_send if step > 0 else tap_left_send
        return hop(
            taps_ref.at[shard], taps_ref.at[shard], send.at[shard], tap_recv.at[shard], step
        )

    def right_hop(o):
        return hop(right_ref.at[o], from_left_ref.at[o], right_send.at[o], right_recv.at[o], 1)

    def left_hop(o):
        return hop(left_ref.at[o], from_right_ref.at[o], left_send.at[o], left_recv.at[o], -1)

    own_taps = pltpu.make_async_copy(filters_ref, taps_ref.at[me], own_sem)
    own_taps.start()
    barrier = pltpu.get_barrier_semaphore()

    @pl.when(has_left)
    def _():
        pl.semaphore_signal(
            barrier, inc=1, device_id={"seq": me - 1}, device_id_type=pl.DeviceIdType.MESH
        )

    @pl.when(has_right)
    def _():
        pl.semaphore_signal(
            barrier, inc=1, device_id={"seq": me + 1}, device_id_type=pl.DeviceIdType.MESH
        )

    source = [sources_ref[w] for w in range(WIN)]
    holders = [owner_ref[k] for k in range(stretches)]
    source_owner = [
        sum(jnp.where(source[w] == k, holders[k], 0) for k in range(stretches)) for w in range(WIN)
    ]
    source_slot = [jnp.int32(0)] * WIN
    slot_stretch = [jnp.int32(0)] * slots
    count = jnp.int32(0)
    for k in range(stretches):
        holder = holders[k]
        for w in range(WIN - 1):
            source_slot[w] += jnp.where((holder == source_owner[w]) & (k < source[w]), 1, 0)
        here = holder == me
        for t in range(slots):
            slot_stretch[t] += jnp.where(here & (count == t), k, 0)
        count += jnp.where(here, 1, 0)
    owners = [jnp.full((STRETCH, 128), source_owner[w], jnp.int32) for w in range(WIN)]

    def choose(mask, yes, no):
        return jnp.where(mask, yes.astype(F32), no.astype(F32))

    first = [
        [last - jnp.maximum(slot_stretch[t] - source[w], -1) for w in range(WIN)]
        for t in range(slots)
    ]

    def gated(slot, o):
        at = (slot, slice(None), pl.ds(pl.multiple_of(o * 128, 128), 128))
        return (key_ref[at].astype(F32) * value_ref[at].astype(F32)).astype(BF16)

    own_taps.wait()

    pl.semaphore_wait(barrier, has_left.astype(jnp.int32) + has_right.astype(jnp.int32))

    @pl.when(has_right)
    def _():
        tap_hop(me, 1).start()

    @pl.when(has_left)
    def _():
        tap_hop(me, -1).start()

    @pl.loop(0, octets)
    def _(o):
        for w in range(WIN - 1):
            piece = gated(source_slot[w], o)
            right_ref[o, w] = piece
            left_ref[o, w] = piece

        @pl.when(jnp.logical_not(has_left))
        def _():
            right_hop(o).start()

        @pl.when(jnp.logical_not(has_right))
        def _():
            left_hop(o).start()

    for d in range(1, size):
        @pl.when(me >= d)
        def _():
            tap_hop(me - d, -1).wait_recv()

            @pl.when(has_right)
            def _():
                tap_hop(me - d, 1).start()

        @pl.when(me + d < size)
        def _():
            tap_hop(me + d, 1).wait_recv()

            @pl.when(has_left)
            def _():
                tap_hop(me + d, -1).start()

    turn_filters(taps_ref, padded_ref)

    @pl.loop(0, octets)
    def _(o):
        spans = padded_ref[pl.ds(pl.multiple_of(o * OCT, OCT), OCT), :]
        for g in range(OCT):
            spread = jnp.broadcast_to(spans[g : g + 1, :], (PIECE, width))
            turned = pltpu.roll(spread, width - 15, 1, stride=1, stride_axis=0).astype(BF16)
            for n in range(stretches + 2):
                g_ref[g, n] = turned[:, 128 * n : 128 * (n + 1)]

        @pl.when(has_left)
        def _():
            right_hop(o).wait_recv()
            for w in range(WIN - 1):
                right_ref[o, w] = choose(
                    owners[w] == me, right_ref[o, w], from_left_ref[o, w]
                ).astype(BF16)

            @pl.when(has_right)
            def _():
                right_hop(o).start()

        @pl.when(has_right)
        def _():
            left_hop(o).wait_recv()
            for w in range(WIN - 1):
                left_ref[o, w] = choose(
                    owners[w] == me, left_ref[o, w], from_right_ref[o, w]
                ).astype(BF16)

            @pl.when(has_left)
            def _():
                left_hop(o).start()

        pieces = []
        for w in range(WIN):
            if w == WIN - 1:
                rows = gated(slots - 1, o)
                rows = choose(owners[w] == me, rows, jnp.zeros_like(rows))
            else:
                rows = choose(owners[w] <= me, right_ref[o, w], left_ref[o, w])
            pieces.append(
                block_transpose([rows[PIECE * e : PIECE * (e + 1), :] for e in range(OCT)])
            )
        results = []
        for g in range(OCT):
            columns = jnp.concatenate(
                [unrolled_columns(pieces[w][g]) for w in range(WIN)], axis=0
            )
            taps = jnp.concatenate(
                [
                    jnp.concatenate(
                        [g_ref[g, first[t][w] + half] for w in range(WIN) for half in range(2)],
                        axis=1,
                    )
                    for t in range(slots)
                ],
                axis=0,
            )
            results.append(jnp.dot(taps, columns, preferred_element_type=F32))
        lanes = pl.ds(pl.multiple_of(o * 128, 128), 128)
        for t in range(slots):
            rows = block_transpose(
                [results[g][PIECE * t : PIECE * (t + 1), :] for g in range(OCT)]
            )
            for a in range(OCT):
                at = (slice(STRETCH * t + PIECE * a, STRETCH * t + PIECE * (a + 1)), lanes)
                out_ref[at] = (query_ref[at].astype(F32) * rows[a]).astype(BF16)

    for shard in range(size):
        @pl.when(has_right & (me >= shard))
        def _():
            tap_hop(shard, 1).wait_send()

        @pl.when(has_left & (me <= shard))
        def _():
            tap_hop(shard, -1).wait_send()

    @pl.loop(0, octets)
    def _(o):
        @pl.when(has_right)
        def _():
            right_hop(o).wait_send()

        @pl.when(has_left)
        def _():
            left_hop(o).wait_send()


def shards(size, key_proj, value_proj, query_proj, filters, sources, owner):
    rows, channels = key_proj.shape
    groups, span = filters.shape
    stretches = owner.shape[0]
    octets = channels // 128
    lags = size * span
    by_slot = (rows // STRETCH, STRETCH, channels)
    key_proj, value_proj = key_proj.reshape(by_slot), value_proj.reshape(by_slot)
    vmem = pl.BlockSpec(memory_space=pltpu.VMEM)
    smem = pl.BlockSpec(memory_space=pltpu.SMEM)
    chunk = pltpu.VMEM((octets, WIN - 1, STRETCH, 128), BF16)
    dma = pltpu.SemaphoreType.DMA
    return pl.pallas_call(
        functools.partial(fused_kernel, size),
        out_shape=jax.ShapeDtypeStruct((rows, channels), BF16),
        in_specs=[smem, smem, vmem, vmem, vmem, vmem],
        out_specs=vmem,
        scratch_shapes=[
            chunk, chunk, chunk, chunk,
            pltpu.VMEM((size, groups, span), BF16),
            pltpu.VMEM((groups, lags + 256), F32),
            pltpu.VMEM((OCT, stretches + 2, PIECE, 128), BF16),
            dma, dma((size,)), dma((size,)), dma((size,)),
            dma((octets,)), dma((octets,)), dma((octets,)), dma((octets,)),
        ],
        compiler_params=pltpu.CompilerParams(
            vmem_limit_bytes=48 * 2**20, collective_id=0, has_side_effects=True
        ),
    )(sources, owner, key_proj, value_proj, query_proj, filters)


def solution(mesh):
    return jax.shard_map(
        functools.partial(shards, mesh.shape["seq"]),
        mesh=mesh,
        in_specs=(
            P(("rep", "seq"), "ch"),
            P(("rep", "seq"), "ch"),
            P(("rep", "seq"), "ch"),
            P("ch", "seq"),
            P("rep"),
            P("rep"),
        ),
        out_specs=P(("rep", "seq"), "ch"),
        check_vma=False,
    )
```

time: 92 us -> 91.6 us (level)
  Pallas kernels: 11.9 us -> 85.1 us
  waiting for transfers between devices: 31.1 us -> 0 us
  blocking collectives: 17.3 us -> 0 us
  between operations: 17.1 us -> 0.02 us
  other arithmetic: 10.3 us -> 0 us
  local copies, waits for them, and re-layouts: 3.92 us -> 6.15 us
    pallas_call x1, Pallas kernels: 11.9 us -> 85.1 us  [shards(): pl.pallas_call(functools.partial(fused_kernel, size), out_shape=jax.Shape...]
    psum x1 -> x0, waiting for transfers between devices: 31.1 us -> none  [shards(): window = lax.psum(jnp.stack(parts), 'seq')]
    all_gather x1 -> x0, blocking collectives: 17.3 us -> none  [shards(): lag_values = lax.all_gather(filters, 'seq', axis=1, tiled=True)]
    reduce_sum x3 -> x0, other arithmetic: 7.63 us -> none  [the longest x2 5.71 us: shards(): jnp.sum(jnp.where((owner == source_owner) & (numbers < source), 1, 0))]
    unnamed x14 -> x13, local copies, waits for them, and re-layouts: 3.27 us -> 6.15 us
    another operation x2 -> x0, other arithmetic: 2.71 us -> none  [shards(): window = lax.psum(jnp.stack(parts), 'seq')]
  transfers between devices with their start and end apart: 1 -> 0, of which waited for: 1 -> 0; matrix products, arithmetic and copies ran while one was open for 0% -> 0% of each run, Pallas kernels for 0% -> 0%
where the time goes in v2:
time: 91.6 us; the launch traced here: 91.3 us
  Pallas kernels  85.1 us (93%)
  local copies, waits for them, and re-layouts  6.15 us (7%)
    pallas_call x1, Pallas kernels, shards(): pl.pallas_call(functools.partial(fused_kernel, size), out_shape=jax.Shape...  85.1 us
    unnamed x13, local copies, waits for them, and re-layouts  6.15 us

profile of v2, /device:TPU:0, one launch (start us, length us, event | category | flops | bytes accessed | tf_op | source)
XLA Modules:
  0.0 91.3 jit_solution(5388212766178367992)
XLA Ops:
  0.0 0.0 copy-start.4
  0.0 0.0 copy-start.5
  0.0 0.7 copy-done.4
  0.7 0.0 copy-done.5
  0.7 0.0 copy-start
  0.7 1.2 %copy-done = bf16[512,1024]{1,0:T(8,128)(2,1)S(1)} copy-done((bf16[512,1024]{1,0:T(8,128)(2,1)S(1)}, bf16[512,1024]{1,0:T(8,128)(2,1)}, u32[]{:S(2)}) %copy-start) | copy-done | bytes 1048600
  1.9 0.0 copy-start.1
  1.9 1.2 %copy-done.1 = bf16[512,1024]{1,0:T(8,128)(2,1)S(1)} copy-done((bf16[512,1024]{1,0:T(8,128)(2,1)S(1)}, bf16[512,1024]{1,0:T(8,128)(2,1)}, u32[]{:S(2)}) %copy-start.1) | copy-done | bytes 1048600
  3.1 0.0 copy-start.2
  3.1 1.2 %copy-done.2 = bf16[512,1024]{1,0:T(8,128)(2,1)S(1)} copy-done((bf16[512,1024]{1,0:T(8,128)(2,1)S(1)}, bf16[512,1024]{1,0:T(8,128)(2,1)}, u32[]{:S(2)}) %copy-start.2) | copy-done | bytes 1048600
  4.3 0.0 copy-start.3
  4.3 0.8 copy-done.3
  5.2 85.1 %shard_map.64 = bf16[512,1024]{1,0:T(8,128)(2,1)S(1)} custom-call(s32[4]{0:T(128)S(1)} %copy-done.4, s32[16]{0:T(128)S(1)} %copy-done.5, bf16[4,128,1024]{2,1,0:T(8,128)(2,1)S(1)} %bitcast.2, bf16[4,128,1024]{2,1,0:T(8,128)(2,1)S(1)} %bitcast.3, bf16[512,1024]{1,0:T(8,128)(2,1)S(1)} %copy-done.2, bf16[64,512]{1,0:T(8,128)(2,1)S(1)} %copy-done.3), custom_call_target="tpu_custom_call" | custom-call | tf_op jit(solution)/shard_map/pallas_call | solution.py:287
  90.3 1.0 %copy.8 = bf16[512,1024]{1,0:T(8,128)(2,1)} copy(bf16[512,1024]{1,0:T(8,128)(2,1)S(1)} %shard_map.64) | data formatting | bytes 2097152
Async XLA Ops:
  0.0 0.7 copy-start.4
  0.0 0.7 copy-start.5
  0.7 1.2 %copy-start = (bf16[512,1024]{1,0:T(8,128)(2,1)S(1)}, bf16[512,1024]{1,0:T(8,128)(2,1)}, u32[]{:S(2)}) copy-start(bf16[512,1024]{1,0:T(8,128)(2,1)} %param.6) | copy-start | bytes 3145732
  1.9 1.2 %copy-start.1 = (bf16[512,1024]{1,0:T(8,128)(2,1)S(1)}, bf16[512,1024]{1,0:T(8,128)(2,1)}, u32[]{:S(2)}) copy-start(bf16[512,1024]{1,0:T(8,128)(2,1)} %param.7) | copy-start | bytes 3145732
  3.1 1.2 %copy-start.2 = (bf16[512,1024]{1,0:T(8,128)(2,1)S(1)}, bf16[512,1024]{1,0:T(8,128)(2,1)}, u32[]{:S(2)}) copy-start(bf16[512,1024]{1,0:T(8,128)(2,1)} %query_ref.1) | copy-start | bytes 3145732
  4.3 0.8 copy-start.3

commit v3 on v2

--- a/solution.py
+++ b/solution.py
@@ -12,6 +12,7 @@
 WIN = 4
 PIECE = 16
 OCT = 8
+AHEAD = 1
 F32 = jnp.float32
 BF16 = jnp.bfloat16
 
@@ -60,9 +61,9 @@
 
 
 def fused_kernel(
-    size, sources_ref, owner_ref, key_ref, value_ref, query_ref, filters_ref,
-    out_ref, right_ref, left_ref, from_left_ref, from_right_ref, taps_ref, padded_ref, g_ref,
-    own_sem, tap_right_send, tap_left_send, tap_recv,
+    size, sources_ref, owner_ref, key_hbm, value_hbm, query_hbm, filters_ref,
+    out_ref, key_ref, value_ref, query_ref, right_ref, left_ref, from_left_ref, from_right_ref, taps_ref, padded_ref, g_ref,
+    own_sem, load_sem, tap_right_send, tap_left_send, tap_recv,
     right_send, right_recv, left_send, left_recv,
 ):
     stretches = owner_ref.shape[0]
@@ -94,6 +95,14 @@
 
     own_taps = pltpu.make_async_copy(filters_ref, taps_ref.at[me], own_sem)
     own_taps.start()
+    loads = [
+        pltpu.make_async_copy(src, dst, load_sem.at[i])
+        for i, (src, dst) in enumerate(
+            ((key_hbm, key_ref), (value_hbm, value_ref), (query_hbm, query_ref))
+        )
+    ]
+    for load in loads:
+        load.start()
     barrier = pltpu.get_barrier_semaphore()
 
     @pl.when(has_left)
@@ -150,6 +159,9 @@
     def _():
         tap_hop(me, -1).start()
 
+    for load in loads:
+        load.wait()
+
     @pl.loop(0, octets)
     def _(o):
         for w in range(WIN - 1):
@@ -157,100 +169,116 @@
             right_ref[o, w] = piece
             left_ref[o, w] = piece
 
-        @pl.when(jnp.logical_not(has_left))
-        def _():
-            right_hop(o).start()
-
-        @pl.when(jnp.logical_not(has_right))
-        def _():
-            left_hop(o).start()
-
-    for d in range(1, size):
-        @pl.when(me >= d)
-        def _():
-            tap_hop(me - d, -1).wait_recv()
+    right_lag = me
+    left_lag = size - 1 - me
+    lag = jnp.maximum(right_lag, left_lag)
+
+    @pl.loop(0, octets + size - 1)
+    def _(s):
+        @pl.when((s >= 1) & (me >= s))
+        def _():
+            tap_hop(me - s, -1).wait_recv()
 
             @pl.when(has_right)
             def _():
-                tap_hop(me - d, 1).start()
-
-        @pl.when(me + d < size)
-        def _():
-            tap_hop(me + d, 1).wait_recv()
+                tap_hop(me - s, 1).start()
+
+        @pl.when((s >= 1) & (me + s < size))
+        def _():
+            tap_hop(me + s, 1).wait_recv()
 
             @pl.when(has_left)
             def _():
-                tap_hop(me + d, -1).start()
-
-    turn_filters(taps_ref, padded_ref)
-
-    @pl.loop(0, octets)
-    def _(o):
-        spans = padded_ref[pl.ds(pl.multiple_of(o * OCT, OCT), OCT), :]
-        for g in range(OCT):
-            spread = jnp.broadcast_to(spans[g : g + 1, :], (PIECE, width))
-            turned = pltpu.roll(spread, width - 15, 1, stride=1, stride_axis=0).astype(BF16)
-            for n in range(stretches + 2):
-                g_ref[g, n] = turned[:, 128 * n : 128 * (n + 1)]
-
-        @pl.when(has_left)
-        def _():
-            right_hop(o).wait_recv()
-            for w in range(WIN - 1):
-                right_ref[o, w] = choose(
-                    owners[w] == me, right_ref[o, w], from_left_ref[o, w]
-                ).astype(BF16)
+                tap_hop(me + s, -1).start()
+
+        @pl.when((s >= right_lag) & (s < right_lag + octets))
+        def _():
+            o = s - right_lag
+
+            @pl.when(has_left)
+            def _():
+                right_hop(o).wait_recv()
+                for w in range(WIN - 1):
+                    right_ref[o, w] = choose(
+                        owners[w] == me, right_ref[o, w], from_left_ref[o, w]
+                    ).astype(BF16)
 
             @pl.when(has_right)
             def _():
+                @pl.when(o >= AHEAD)
+                def _():
+                    right_hop(o - AHEAD).wait_send()
+
                 right_hop(o).start()
 
-        @pl.when(has_right)
-        def _():
-            left_hop(o).wait_recv()
-            for w in range(WIN - 1):
-                left_ref[o, w] = choose(
-                    owners[w] == me, left_ref[o, w], from_right_ref[o, w]
-                ).astype(BF16)
+        @pl.when((s >= left_lag) & (s < left_lag + octets))
+        def _():
+            o = s - left_lag
+
+            @pl.when(has_right)
+            def _():
+                left_hop(o).wait_recv()
+                for w in range(WIN - 1):
+                    left_ref[o, w] = choose(
+                        owners[w] == me, left_ref[o, w], from_right_ref[o, w]
+                    ).astype(BF16)
 
             @pl.when(has_left)
             def _():
+                @pl.when(o >= AHEAD)
+                def _():
+                    left_hop(o - AHEAD).wait_send()
+
                 left_hop(o).start()
 
-        pieces = []
-        for w in range(WIN):
-            if w == WIN - 1:
-                rows = gated(slots - 1, o)
-                rows = choose(owners[w] == me, rows, jnp.zeros_like(rows))
-            else:
-                rows = choose(owners[w] <= me, right_ref[o, w], left_ref[o, w])
-            pieces.append(
-                block_transpose([rows[PIECE * e : PIECE * (e + 1), :] for e in range(OCT)])
-            )
-        results = []
-        for g in range(OCT):
-            columns = jnp.concatenate(
-                [unrolled_columns(pieces[w][g]) for w in range(WIN)], axis=0
-            )
-            taps = jnp.concatenate(
-                [
-                    jnp.concatenate(
-                        [g_ref[g, first[t][w] + half] for w in range(WIN) for half in range(2)],
-                        axis=1,
-                    )
-                    for t in range(slots)
-                ],
-                axis=0,
-            )
-            results.append(jnp.dot(taps, columns, preferred_element_type=F32))
-        lanes = pl.ds(pl.multiple_of(o * 128, 128), 128)
-        for t in range(slots):
-            rows = block_transpose(
-                [results[g][PIECE * t : PIECE * (t + 1), :] for g in range(OCT)]
-            )
-            for a in range(OCT):
-                at = (slice(STRETCH * t + PIECE * a, STRETCH * t + PIECE * (a + 1)), lanes)
-                out_ref[at] = (query_ref[at].astype(F32) * rows[a]).astype(BF16)
+        @pl.when(s == lag)
+        def _():
+            turn_filters(taps_ref, padded_ref)
+
+        @pl.when((s >= lag) & (s < lag + octets))
+        def _():
+            o = s - lag
+            spans = padded_ref[pl.ds(pl.multiple_of(o * OCT, OCT), OCT), :]
+            for g in range(OCT):
+                spread = jnp.broadcast_to(spans[g : g + 1, :], (PIECE, width))
+                turned = pltpu.roll(spread, width - 15, 1, stride=1, stride_axis=0).astype(BF16)
+                for n in range(stretches + 2):
+                    g_ref[g, n] = turned[:, 128 * n : 128 * (n + 1)]
+
+            pieces = []
+            for w in range(WIN):
+                if w == WIN - 1:
+                    rows = gated(slots - 1, o)
+                    rows = choose(owners[w] == me, rows, jnp.zeros_like(rows))
+                else:
+                    rows = choose(owners[w] <= me, right_ref[o, w], left_ref[o, w])
+                pieces.append(
+                    block_transpose([rows[PIECE * e : PIECE * (e + 1), :] for e in range(OCT)])
+                )
+            results = []
+            for g in range(OCT):
+                columns = jnp.concatenate(
+                    [unrolled_columns(pieces[w][g]) for w in range(WIN)], axis=0
+                )
+                taps = jnp.concatenate(
+                    [
+                        jnp.concatenate(
+                            [g_ref[g, first[t][w] + half] for w in range(WIN) for half in range(2)],
+                            axis=1,
+                        )
+                        for t in range(slots)
+                    ],
+                    axis=0,
+                )
+                results.append(jnp.dot(taps, columns, preferred_element_type=F32))
+            lanes = pl.ds(pl.multiple_of(o * 128, 128), 128)
+            for t in range(slots):
+                rows = block_transpose(
+                    [results[g][PIECE * t : PIECE * (t + 1), :] for g in range(OCT)]
+                )
+                for a in range(OCT):
+                    at = (slice(STRETCH * t + PIECE * a, STRETCH * t + PIECE * (a + 1)), lanes)
+                    out_ref[at] = (query_ref[at].astype(F32) * rows[a]).astype(BF16)
 
     for shard in range(size):
         @pl.when(has_right & (me >= shard))
@@ -261,7 +289,7 @@
         def _():
             tap_hop(shard, -1).wait_send()
 
-    @pl.loop(0, octets)
+    @pl.loop(max(octets - AHEAD, 0), octets)
     def _(o):
         @pl.when(has_right)
         def _():
@@ -281,24 +309,26 @@
     by_slot = (rows // STRETCH, STRETCH, channels)
     key_proj, value_proj = key_proj.reshape(by_slot), value_proj.reshape(by_slot)
     vmem = pl.BlockSpec(memory_space=pltpu.VMEM)
+    hbm = pl.BlockSpec(memory_space=pl.ANY)
     smem = pl.BlockSpec(memory_space=pltpu.SMEM)
     chunk = pltpu.VMEM((octets, WIN - 1, STRETCH, 128), BF16)
     dma = pltpu.SemaphoreType.DMA
     return pl.pallas_call(
         functools.partial(fused_kernel, size),
         out_shape=jax.ShapeDtypeStruct((rows, channels), BF16),
-        in_specs=[smem, smem, vmem, vmem, vmem, vmem],
+        in_specs=[smem, smem, hbm, hbm, hbm, hbm],
         out_specs=vmem,
         scratch_shapes=[
+            pltpu.VMEM(by_slot, BF16), pltpu.VMEM(by_slot, BF16), pltpu.VMEM((rows, channels), BF16),
             chunk, chunk, chunk, chunk,
             pltpu.VMEM((size, groups, span), BF16),
             pltpu.VMEM((groups, lags + 256), F32),
             pltpu.VMEM((OCT, stretches + 2, PIECE, 128), BF16),
-            dma, dma((size,)), dma((size,)), dma((size,)),
+            dma, dma((3,)), dma((size,)), dma((size,)), dma((size,)),
             dma((octets,)), dma((octets,)), dma((octets,)), dma((octets,)),
         ],
         compiler_params=pltpu.CompilerParams(
-            vmem_limit_bytes=48 * 2**20, collective_id=0, has_side_effects=True
+            vmem_limit_bytes=60 * 2**20, collective_id=0, has_side_effects=True
         ),
     )(sources, owner, key_proj, value_proj, query_proj, filters)
 

time: 91.6 us -> 50.5 us (0.55)
  Pallas kernels: 85.1 us -> 48.1 us
  local copies, waits for them, and re-layouts: 6.15 us -> 2.26 us
    pallas_call x1, Pallas kernels: 85.1 us -> 48.1 us  [shards(): pl.pallas_call(functools.partial(fused_kernel, size), out_shape=jax.Shape...]
    unnamed x13 -> x1, local copies, waits for them, and re-layouts: 6.15 us -> 2.26 us
where the time goes in v3:
time: 50.5 us; the launch traced here: 50.4 us
  Pallas kernels  48.1 us (95%)
  local copies, waits for them, and re-layouts  2.26 us (4%)
    pallas_call x1, Pallas kernels, shards(): pl.pallas_call(functools.partial(fused_kernel, size), out_shape=jax.Shape...  48.1 us
    unnamed x1, local copies, waits for them, and re-layouts  2.26 us

profile of v3, /device:TPU:0, one launch (start us, length us, event | category | flops | bytes accessed | tf_op | source)
XLA Modules:
  0.0 50.4 jit_solution(11254741469728904911)
XLA Ops:
  0.0 48.1 %shard_map.64 = bf16[512,1024]{1,0:T(8,128)(2,1)} custom-call(s32[4]{0:T(128)} %sources_ref.1, s32[16]{0:T(128)} %owner_ref.1, bf16[4,128,1024]{2,1,0:T(8,128)(2,1)} %bitcast.2, bf16[4,128,1024]{2,1,0:T(8,128)(2,1)} %bitcast.3, bf16[512,1024]{1,0:T(8,128)(2,1)} %query_hbm.1, bf16[64,512]{1,0:T(8,128)(2,1)} %filters_ref.1), custom_call_target="tpu_custom_call" | custom-call | tf_op jit(solution)/shard_map/pallas_call | solution.py:316
  48.1 2.3 %copy.8 = bf16[512,1024]{1,0:T(8,128)(2,1)} copy(bf16[512,1024]{1,0:T(8,128)(2,1)} %shard_map.64) | data formatting | bytes 2097152

commit v4 on v3

--- a/solution.py
+++ b/solution.py
@@ -12,7 +12,9 @@
 WIN = 4
 PIECE = 16
 OCT = 8
-AHEAD = 1
+AHEAD = 8
+HOP = 6
+SENT = WIN - 1
 F32 = jnp.float32
 BF16 = jnp.bfloat16
 
@@ -133,6 +135,13 @@
         for t in range(slots):
             slot_stretch[t] += jnp.where(here & (count == t), k, 0)
         count += jnp.where(here, 1, 0)
+    chunks = octets * SENT
+
+    def is_mine(c):
+        w = c % SENT
+        holder = sum(jnp.where(w == k, source_owner[k], 0) for k in range(SENT))
+        return jnp.full((STRETCH, 128), holder, jnp.int32) == me
+
     owners = [jnp.full((STRETCH, 128), source_owner[w], jnp.int32) for w in range(WIN)]
 
     def choose(mask, yes, no):
@@ -159,49 +168,49 @@
     def _():
         tap_hop(me, -1).start()
 
-    for load in loads:
-        load.wait()
+    loads[0].wait()
+    loads[1].wait()
 
     @pl.loop(0, octets)
     def _(o):
         for w in range(WIN - 1):
             piece = gated(source_slot[w], o)
-            right_ref[o, w] = piece
-            left_ref[o, w] = piece
-
-    right_lag = me
-    left_lag = size - 1 - me
+            right_ref[o * SENT + w] = piece
+            left_ref[o * SENT + w] = piece
+
+    right_lag = HOP * me
+    left_lag = HOP * (size - 1 - me)
     lag = jnp.maximum(right_lag, left_lag)
 
-    @pl.loop(0, octets + size - 1)
+    @pl.loop(0, chunks + HOP * (size - 1))
     def _(s):
-        @pl.when((s >= 1) & (me >= s))
-        def _():
-            tap_hop(me - s, -1).wait_recv()
+        far = s // HOP
+        turn = (s % HOP == 0) & (far >= 1)
+
+        @pl.when(turn & (me >= far))
+        def _():
+            tap_hop(me - far, -1).wait_recv()
 
             @pl.when(has_right)
             def _():
-                tap_hop(me - s, 1).start()
-
-        @pl.when((s >= 1) & (me + s < size))
-        def _():
-            tap_hop(me + s, 1).wait_recv()
+                tap_hop(me - far, 1).start()
+
+        @pl.when(turn & (me + far < size))
+        def _():
+            tap_hop(me + far, 1).wait_recv()
 
             @pl.when(has_left)
             def _():
-                tap_hop(me + s, -1).start()
-
-        @pl.when((s >= right_lag) & (s < right_lag + octets))
+                tap_hop(me + far, -1).start()
+
+        @pl.when((s >= right_lag) & (s < right_lag + chunks))
         def _():
             o = s - right_lag
 
             @pl.when(has_left)
             def _():
                 right_hop(o).wait_recv()
-                for w in range(WIN - 1):
-                    right_ref[o, w] = choose(
-                        owners[w] == me, right_ref[o, w], from_left_ref[o, w]
-                    ).astype(BF16)
+                right_ref[o] = choose(is_mine(o), right_ref[o], from_left_ref[o]).astype(BF16)
 
             @pl.when(has_right)
             def _():
@@ -211,17 +220,14 @@
 
                 right_hop(o).start()
 
-        @pl.when((s >= left_lag) & (s < left_lag + octets))
+        @pl.when((s >= left_lag) & (s < left_lag + chunks))
         def _():
             o = s - left_lag
 
             @pl.when(has_right)
             def _():
                 left_hop(o).wait_recv()
-                for w in range(WIN - 1):
-                    left_ref[o, w] = choose(
-                        owners[w] == me, left_ref[o, w], from_right_ref[o, w]
-                    ).astype(BF16)
+                left_ref[o] = choose(is_mine(o), left_ref[o], from_right_ref[o]).astype(BF16)
 
             @pl.when(has_left)
             def _():
@@ -234,10 +240,11 @@
         @pl.when(s == lag)
         def _():
             turn_filters(taps_ref, padded_ref)
-
-        @pl.when((s >= lag) & (s < lag + octets))
-        def _():
-            o = s - lag
+            loads[2].wait()
+
+        @pl.when((s >= lag) & (s < lag + chunks) & ((s - lag) % SENT == SENT - 1))
+        def _():
+            o = (s - lag) // SENT
             spans = padded_ref[pl.ds(pl.multiple_of(o * OCT, OCT), OCT), :]
             for g in range(OCT):
                 spread = jnp.broadcast_to(spans[g : g + 1, :], (PIECE, width))
@@ -251,7 +258,7 @@
                     rows = gated(slots - 1, o)
                     rows = choose(owners[w] == me, rows, jnp.zeros_like(rows))
                 else:
-                    rows = choose(owners[w] <= me, right_ref[o, w], left_ref[o, w])
+                    rows = choose(owners[w] <= me, right_ref[o * SENT + w], left_ref[o * SENT + w])
                 pieces.append(
                     block_transpose([rows[PIECE * e : PIECE * (e + 1), :] for e in range(OCT)])
                 )
@@ -289,7 +296,7 @@
         def _():
             tap_hop(shard, -1).wait_send()
 
-    @pl.loop(max(octets - AHEAD, 0), octets)
+    @pl.loop(max(chunks - AHEAD, 0), chunks)
     def _(o):
         @pl.when(has_right)
         def _():
@@ -306,12 +313,13 @@
     stretches = owner.shape[0]
     octets = channels // 128
     lags = size * span
+    chunks = octets * SENT
     by_slot = (rows // STRETCH, STRETCH, channels)
     key_proj, value_proj = key_proj.reshape(by_slot), value_proj.reshape(by_slot)
     vmem = pl.BlockSpec(memory_space=pltpu.VMEM)
     hbm = pl.BlockSpec(memory_space=pl.ANY)
     smem = pl.BlockSpec(memory_space=pltpu.SMEM)
-    chunk = pltpu.VMEM((octets, WIN - 1, STRETCH, 128), BF16)
+    chunk = pltpu.VMEM((chunks, STRETCH, 128), BF16)
     dma = pltpu.SemaphoreType.DMA
     return pl.pallas_call(
         functools.partial(fused_kernel, size),
@@ -325,10 +333,10 @@
             pltpu.VMEM((groups, lags + 256), F32),
             pltpu.VMEM((OCT, stretches + 2, PIECE, 128), BF16),
             dma, dma((3,)), dma((size,)), dma((size,)), dma((size,)),
-            dma((octets,)), dma((octets,)), dma((octets,)), dma((octets,)),
+            dma((chunks,)), dma((chunks,)), dma((chunks,)), dma((chunks,)),
         ],
         compiler_params=pltpu.CompilerParams(
-            vmem_limit_bytes=60 * 2**20, collective_id=0, has_side_effects=True
+            vmem_limit_bytes=40 * 2**20, collective_id=0, has_side_effects=True
         ),
     )(sources, owner, key_proj, value_proj, query_proj, filters)
 

time: 50.5 us -> 42 us (0.83)
  Pallas kernels: 48.1 us -> 35.5 us
  local copies, waits for them, and re-layouts: 2.26 us -> 6.15 us
    pallas_call x1, Pallas kernels: 48.1 us -> 35.5 us  [shards(): pl.pallas_call(functools.partial(fused_kernel, size), out_shape=jax.Shape...]
    unnamed x1 -> x13, local copies, waits for them, and re-layouts: 2.26 us -> 6.15 us
where the time goes in v4:
time: 42 us; the launch traced here: 41.7 us
  Pallas kernels  35.5 us (85%)
  local copies, waits for them, and re-layouts  6.15 us (15%)
    pallas_call x1, Pallas kernels, shards(): pl.pallas_call(functools.partial(fused_kernel, size), out_shape=jax.Shape...  35.5 us
    unnamed x13, local copies, waits for them, and re-layouts  6.15 us

profile of v4, /device:TPU:0, one launch (start us, length us, event | category | flops | bytes accessed | tf_op | source)
XLA Modules:
  0.0 41.7 jit_solution(7964186179896093109)
XLA Ops:
  0.0 0.0 copy-start.4
  0.0 0.0 copy-start.5
  0.0 0.7 %copy-done.4 = s32[4]{0:T(128)S(1)} copy-done((s32[4]{0:T(128)S(1)}, s32[4]{0:T(128)}, u32[]{:S(2)}) %copy-start.4) | copy-done | bytes 40
  0.7 0.0 copy-done.5
  0.7 0.0 copy-start
  0.7 1.2 %copy-done = bf16[512,1024]{1,0:T(8,128)(2,1)S(1)} copy-done((bf16[512,1024]{1,0:T(8,128)(2,1)S(1)}, bf16[512,1024]{1,0:T(8,128)(2,1)}, u32[]{:S(2)}) %copy-start) | copy-done | bytes 1048600
  1.9 0.0 copy-start.1
  1.9 1.2 %copy-done.1 = bf16[512,1024]{1,0:T(8,128)(2,1)S(1)} copy-done((bf16[512,1024]{1,0:T(8,128)(2,1)S(1)}, bf16[512,1024]{1,0:T(8,128)(2,1)}, u32[]{:S(2)}) %copy-start.1) | copy-done | bytes 1048600
  3.1 0.0 copy-start.2
  3.1 1.2 %copy-done.2 = bf16[512,1024]{1,0:T(8,128)(2,1)S(1)} copy-done((bf16[512,1024]{1,0:T(8,128)(2,1)S(1)}, bf16[512,1024]{1,0:T(8,128)(2,1)}, u32[]{:S(2)}) %copy-start.2) | copy-done | bytes 1048600
  4.3 0.0 copy-start.3
  4.3 0.8 %copy-done.3 = bf16[64,512]{1,0:T(8,128)(2,1)S(1)} copy-done((bf16[64,512]{1,0:T(8,128)(2,1)S(1)}, bf16[64,512]{1,0:T(8,128)(2,1)}, u32[]{:S(2)}) %copy-start.3) | copy-done | bytes 65560
  5.2 35.5 %shard_map.64 = bf16[512,1024]{1,0:T(8,128)(2,1)S(1)} custom-call(s32[4]{0:T(128)S(1)} %copy-done.4, s32[16]{0:T(128)S(1)} %copy-done.5, bf16[4,128,1024]{2,1,0:T(8,128)(2,1)S(1)} %bitcast.2, bf16[4,128,1024]{2,1,0:T(8,128)(2,1)S(1)} %bitcast.3, bf16[512,1024]{1,0:T(8,128)(2,1)S(1)} %copy-done.2, bf16[64,512]{1,0:T(8,128)(2,1)S(1)} %copy-done.3), custom_call_target="tpu_custom_call" | custom-call | tf_op jit(solution)/shard_map/pallas_call | solution.py:324
  40.7 1.0 %copy.8 = bf16[512,1024]{1,0:T(8,128)(2,1)} copy(bf16[512,1024]{1,0:T(8,128)(2,1)S(1)} %shard_map.64) | data formatting | bytes 2097152
Async XLA Ops:
  0.0 0.7 %copy-start.4 = (s32[4]{0:T(128)S(1)}, s32[4]{0:T(128)}, u32[]{:S(2)}) copy-start(s32[4]{0:T(128)} %sources_ref.1) | copy-start | bytes 52
  0.0 0.7 %copy-start.5 = (s32[16]{0:T(128)S(1)}, s32[16]{0:T(128)}, u32[]{:S(2)}) copy-start(s32[16]{0:T(128)} %owner_ref.1) | copy-start | bytes 196
  0.7 1.2 %copy-start = (bf16[512,1024]{1,0:T(8,128)(2,1)S(1)}, bf16[512,1024]{1,0:T(8,128)(2,1)}, u32[]{:S(2)}) copy-start(bf16[512,1024]{1,0:T(8,128)(2,1)} %param.6) | copy-start | bytes 3145732
  1.9 1.2 %copy-start.1 = (bf16[512,1024]{1,0:T(8,128)(2,1)S(1)}, bf16[512,1024]{1,0:T(8,128)(2,1)}, u32[]{:S(2)}) copy-start(bf16[512,1024]{1,0:T(8,128)(2,1)} %param.7) | copy-start | bytes 3145732
  3.1 1.2 %copy-start.2 = (bf16[512,1024]{1,0:T(8,128)(2,1)S(1)}, bf16[512,1024]{1,0:T(8,128)(2,1)}, u32[]{:S(2)}) copy-start(bf16[512,1024]{1,0:T(8,128)(2,1)} %query_hbm.1) | copy-start | bytes 3145732
  4.3 0.8 %copy-start.3 = (bf16[64,512]{1,0:T(8,128)(2,1)S(1)}, bf16[64,512]{1,0:T(8,128)(2,1)}, u32[]{:S(2)}) copy-start(bf16[64,512]{1,0:T(8,128)(2,1)} %filters_ref.1) | copy-start | bytes 196612

commit v5 on v4

--- a/solution.py
+++ b/solution.py
@@ -40,11 +40,11 @@
 def unrolled_columns(piece):
     block = lane_block(PIECE)
     rows = [None] * 16
-    zero = jnp.zeros_like(piece)
     for j in range(OCT):
         turned = pltpu.roll(piece, PIECE * j, 1) if j else piece
-        rows[7 - j] = jnp.where(block >= j, turned, zero).astype(BF16)
-        rows[15 - j] = jnp.where(block < j, turned, zero).astype(BF16)
+        turned = turned.astype(BF16)
+        rows[7 - j] = turned * jnp.where(block >= j, 1.0, 0.0).astype(BF16)
+        rows[15 - j] = turned * jnp.where(block < j, 1.0, 0.0).astype(BF16)
     return jnp.concatenate(rows, axis=0)
 
 

time: 42 us -> 41.9 us (level)
  no operation moved by 1% of the time
where the time goes in v5:
time: 41.9 us; the launch traced here: 41.7 us
  Pallas kernels  35.5 us (85%)
  local copies, waits for them, and re-layouts  6.15 us (15%)
    pallas_call x1, Pallas kernels, shards(): pl.pallas_call(functools.partial(fused_kernel, size), out_shape=jax.Shape...  35.5 us
    unnamed x13, local copies, waits for them, and re-layouts  6.15 us

profile of v5, /device:TPU:0, one launch (start us, length us, event | category | flops | bytes accessed | tf_op | source)
XLA Modules:
  0.0 41.7 jit_solution(10996881977939627056)
XLA Ops:
  0.0 0.0 copy-start.4
  0.0 0.0 copy-start.5
  0.0 0.7 %copy-done.4 = s32[4]{0:T(128)S(1)} copy-done((s32[4]{0:T(128)S(1)}, s32[4]{0:T(128)}, u32[]{:S(2)}) %copy-start.4) | copy-done | bytes 40
  0.7 0.0 copy-done.5
  0.7 0.0 copy-start
  0.7 1.2 %copy-done = bf16[512,1024]{1,0:T(8,128)(2,1)S(1)} copy-done((bf16[512,1024]{1,0:T(8,128)(2,1)S(1)}, bf16[512,1024]{1,0:T(8,128)(2,1)}, u32[]{:S(2)}) %copy-start) | copy-done | bytes 1048600
  1.9 0.0 copy-start.1
  1.9 1.2 %copy-done.1 = bf16[512,1024]{1,0:T(8,128)(2,1)S(1)} copy-done((bf16[512,1024]{1,0:T(8,128)(2,1)S(1)}, bf16[512,1024]{1,0:T(8,128)(2,1)}, u32[]{:S(2)}) %copy-start.1) | copy-done | bytes 1048600
  3.1 0.0 copy-start.2
  3.1 1.2 %copy-done.2 = bf16[512,1024]{1,0:T(8,128)(2,1)S(1)} copy-done((bf16[512,1024]{1,0:T(8,128)(2,1)S(1)}, bf16[512,1024]{1,0:T(8,128)(2,1)}, u32[]{:S(2)}) %copy-start.2) | copy-done | bytes 1048600
  4.3 0.0 copy-start.3
  4.3 0.8 %copy-done.3 = bf16[64,512]{1,0:T(8,128)(2,1)S(1)} copy-done((bf16[64,512]{1,0:T(8,128)(2,1)S(1)}, bf16[64,512]{1,0:T(8,128)(2,1)}, u32[]{:S(2)}) %copy-start.3) | copy-done | bytes 65560
  5.2 35.5 %shard_map.64 = bf16[512,1024]{1,0:T(8,128)(2,1)S(1)} custom-call(s32[4]{0:T(128)S(1)} %copy-done.4, s32[16]{0:T(128)S(1)} %copy-done.5, bf16[4,128,1024]{2,1,0:T(8,128)(2,1)S(1)} %bitcast.2, bf16[4,128,1024]{2,1,0:T(8,128)(2,1)S(1)} %bitcast.3, bf16[512,1024]{1,0:T(8,128)(2,1)S(1)} %copy-done.2, bf16[64,512]{1,0:T(8,128)(2,1)S(1)} %copy-done.3), custom_call_target="tpu_custom_call" | custom-call | tf_op jit(solution)/shard_map/pallas_call | solution.py:324
  40.7 1.0 %copy.8 = bf16[512,1024]{1,0:T(8,128)(2,1)} copy(bf16[512,1024]{1,0:T(8,128)(2,1)S(1)} %shard_map.64) | data formatting | bytes 2097152
Async XLA Ops:
  0.0 0.7 %copy-start.4 = (s32[4]{0:T(128)S(1)}, s32[4]{0:T(128)}, u32[]{:S(2)}) copy-start(s32[4]{0:T(128)} %sources_ref.1) | copy-start | bytes 52
  0.0 0.7 %copy-start.5 = (s32[16]{0:T(128)S(1)}, s32[16]{0:T(128)}, u32[]{:S(2)}) copy-start(s32[16]{0:T(128)} %owner_ref.1) | copy-start | bytes 196
  0.7 1.2 %copy-start = (bf16[512,1024]{1,0:T(8,128)(2,1)S(1)}, bf16[512,1024]{1,0:T(8,128)(2,1)}, u32[]{:S(2)}) copy-start(bf16[512,1024]{1,0:T(8,128)(2,1)} %param.6) | copy-start | bytes 3145732
  1.9 1.2 %copy-start.1 = (bf16[512,1024]{1,0:T(8,128)(2,1)S(1)}, bf16[512,1024]{1,0:T(8,128)(2,1)}, u32[]{:S(2)}) copy-start(bf16[512,1024]{1,0:T(8,128)(2,1)} %param.7) | copy-start | bytes 3145732
  3.1 1.2 %copy-start.2 = (bf16[512,1024]{1,0:T(8,128)(2,1)S(1)}, bf16[512,1024]{1,0:T(8,128)(2,1)}, u32[]{:S(2)}) copy-start(bf16[512,1024]{1,0:T(8,128)(2,1)} %query_hbm.1) | copy-start | bytes 3145732
  4.3 0.8 %copy-start.3 = (bf16[64,512]{1,0:T(8,128)(2,1)S(1)}, bf16[64,512]{1,0:T(8,128)(2,1)}, u32[]{:S(2)}) copy-start(bf16[64,512]{1,0:T(8,128)(2,1)} %filters_ref.1) | copy-start | bytes 196612
